TPU v7x, 32 devices: a whole 2x2x4 slice. The times are simulated.
32 devices in a mesh: dp: 8 (over z, y), tensor: 4 (over x, core).
Axes of the slice: x: 2, y: 2, z: 4, core: 2. Of those that a mesh axis runs over, the one named last changes fastest.
Arguments:
- activations: bfloat16 [2048, 8192], P('dp'), may hold values from -6 to 6
- key_value_grads: bfloat16 [2048, 2, 1024], P('dp', None, 'tensor'), may hold values from -6 to 6
- owner_table: int32 [64], replicated, may hold values from 0 to 63, each once
- left_factors: float32 [4, 64, 512, 512], P('tensor', 'dp'), may hold values from -16 to 16, as said below
- right_factors: float32 [4, 64, 128, 128], P('tensor', 'dp'), may hold values from -16 to 16, as said below
Outputs:
- left_updated: float32 [4, 64, 512, 512], P('tensor', 'dp')
- right_updated: float32 [4, 64, 128, 128], P('tensor', 'dp')
- update: bfloat16 [2, 8192, 1024], P(None, 'dp')
Inputs may be any that keep to these rules, and one draw needn't show every extreme that they name: `owner_table`: each block number appears once; slot s lies on index s // 8 of dp. `left_factors`: every block is symmetric positive definite. `right_factors`: every block is symmetric positive definite.
All inputs are finite; a program needn't handle non-finite values.
Results may differ from a plain program's by a relative error of at most 0.012.
The roundings to bfloat16 on the way count: a program that leaves them out, or rounds other values in their place, can miss the bound.
Values may be sent and summed in bfloat16 or wider, within the bound.
A program may use at most 128 MiB of HBM per device.

v0:
```python
import functools

import jax
import jax.numpy as jnp
from jax import lax
from jax.experimental import pallas as pl
from jax.experimental.pallas import tpu as pltpu
from jax.sharding import PartitionSpec as P

ITERS = 8
MOMENT_DECAY = 0.9
RIDGE_SHARE = 0.0001
CHUNK_SLOTS = 2
VMEM_LIMIT = 60 * 1024 * 1024


def dot(left_mat, right_mat):
    return jnp.dot(left_mat, right_mat, preferred_element_type=jnp.float32)


def halves(x):
    high = x.astype(jnp.bfloat16)
    low = (x - high.astype(jnp.float32)).astype(jnp.bfloat16)
    return high, low


def gradient_kernel(
    table_ref, act_ref, kv_ref, out_ref, *, chunk, chunk_slots, slots, per_projection, col_blocks, scale
):
    rows_block, cols_block = out_ref.shape[2:]
    width = col_blocks * cols_block
    first = pl.program_id(0) * slots + chunk * chunk_slots
    for k in range(chunk_slots):
        block_id = table_ref[first + k]
        projection = block_id // per_projection
        remainder = block_id % per_projection
        row_start = pl.multiple_of(remainder // col_blocks * rows_block, rows_block)
        col_start = pl.multiple_of(
            projection * width + remainder % col_blocks * cols_block, cols_block
        )
        summed = lax.dot_general(
            act_ref[:, pl.ds(row_start, rows_block)],
            kv_ref[:, pl.ds(col_start, cols_block)],
            (((0,), (0,)), ((), ())),
            preferred_element_type=jnp.float32,
        )
        out_ref[0, k] = summed * scale


def gradient_chunk(table, activations, cotangents, chunk, chunk_slots, ranks, rows_block, cols_block, col_blocks):
    tokens, model = activations.shape
    slots = table.shape[0] // ranks
    body = functools.partial(
        gradient_kernel,
        chunk=chunk,
        chunk_slots=chunk_slots,
        slots=slots,
        per_projection=model // rows_block * col_blocks,
        col_blocks=col_blocks,
        scale=1.0 / (tokens * ranks),
    )
    return pl.pallas_call(
        body,
        out_shape=jax.ShapeDtypeStruct((ranks, chunk_slots, rows_block, cols_block), jnp.float32),
        grid_spec=pltpu.PrefetchScalarGridSpec(
            num_scalar_prefetch=1,
            grid=(ranks,),
            in_specs=[
                pl.BlockSpec(activations.shape, lambda d, t: (0, 0), pipeline_mode=pl.Buffered(1)),
                pl.BlockSpec(cotangents.shape, lambda d, t: (0, 0), pipeline_mode=pl.Buffered(1)),
            ],
            out_specs=pl.BlockSpec(
                (1, chunk_slots, rows_block, cols_block), lambda d, t: (d, 0, 0, 0)
            ),
        ),
        compiler_params=pltpu.CompilerParams(vmem_limit_bytes=VMEM_LIMIT),
        cost_estimate=pl.CostEstimate(
            flops=2 * ranks * chunk_slots * rows_block * cols_block * tokens,
            bytes_accessed=activations.size * 2 + ranks * chunk_slots * rows_block * cols_block * 4,
            transcendentals=0,
        ),
    )(table, activations, cotangents)


def diagonal(order):
    rows = lax.broadcasted_iota(jnp.int32, (order, order), 0)
    return rows == lax.broadcasted_iota(jnp.int32, (order, order), 1)


def total(x):
    return jnp.sum(jnp.sum(x, axis=1, keepdims=True), axis=0, keepdims=True)


def factor_of(powered, on_diagonal):
    return ((jnp.where(on_diagonal, 5.0, 0.0) - powered) * 0.25).astype(jnp.bfloat16)


def begin_root(updated, m_ref, f_ref, x_ref):
    order = updated.shape[0]
    on_diagonal = diagonal(order)
    trace = total(jnp.where(on_diagonal, updated, 0.0))
    shifted = updated + jnp.where(on_diagonal, RIDGE_SHARE * trace / order, 0.0)
    scaling = 2.5 / jnp.sqrt(total(shifted * shifted))
    powered = scaling * shifted
    factor = factor_of(powered, on_diagonal)
    start = jnp.sqrt(jnp.sqrt(scaling)).astype(jnp.bfloat16).astype(jnp.float32)
    m_ref[...] = powered.astype(jnp.bfloat16)
    f_ref[...] = factor
    x_ref[...] = start * factor.astype(jnp.float32)


def root_steps(groups):
    squares = []
    for m_ref, f_ref, x_ref in groups:
        factor = f_ref[...]
        squares.append(dot(factor, factor).astype(jnp.bfloat16))
    fourths = [dot(s, s).astype(jnp.bfloat16) for s in squares]
    for fourth, (m_ref, f_ref, x_ref) in zip(fourths, groups):
        powered = dot(fourth, m_ref[...])
        m_ref[...] = powered.astype(jnp.bfloat16)
        f_ref[...] = factor_of(powered, diagonal(powered.shape[0]))
    for m_ref, f_ref, x_ref in groups:
        x_ref[...] = dot(x_ref[...].astype(jnp.bfloat16), f_ref[...])


def block_kernel(grad_ref, left_ref, right_ref, *rest, chunk_slots, chained):
    if chained:
        rest = rest[2:]
    left_out, right_out, dir_ref, ml, fl, xl, mr, fr, xr = rest
    groups = []
    for k in range(chunk_slots):
        grad = grad_ref[k]
        high, low = halves(grad)
        flipped = grad.T
        high_t, low_t = halves(flipped)
        wide = jnp.concatenate([high, high, low], axis=1)
        wide_t = jnp.concatenate([high_t, high_t, low_t], axis=1)
        tall = jnp.concatenate([high, low, high], axis=0)
        tall_t = jnp.concatenate([high_t, low_t, high_t], axis=0)
        left_new = MOMENT_DECAY * left_ref[k] + (1.0 - MOMENT_DECAY) * dot(wide, tall_t)
        right_new = MOMENT_DECAY * right_ref[k] + (1.0 - MOMENT_DECAY) * dot(wide_t, tall)
        left_out[k] = left_new
        right_out[k] = right_new
        begin_root(left_new, ml.at[k], fl.at[k], xl.at[k])
        begin_root(right_new, mr.at[k], fr.at[k], xr.at[k])
        groups.append((ml.at[k], fl.at[k], xl.at[k]))
        groups.append((mr.at[k], fr.at[k], xr.at[k]))

    def step(_, carry):
        root_steps(groups)
        return carry

    lax.fori_loop(0, ITERS - 1, step, 0)
    for k in range(chunk_slots):
        high, low = halves(grad_ref[k])
        tall = jnp.concatenate([high, low, high], axis=0)
        root_high, root_low = halves(xl[k])
        half = dot(jnp.concatenate([root_high, root_high, root_low], axis=1), tall)
        half_high, half_low = halves(half)
        right_high, right_low = halves(xr[k])
        precond = dot(
            jnp.concatenate([half_high, half_high, half_low], axis=1),
            jnp.concatenate([right_high, right_low, right_high], axis=0),
        )
        mean = total(precond * precond) / precond.size
        dir_ref[k] = (precond / jnp.sqrt(mean + 1e-06)).astype(jnp.bfloat16)


def block_chunk(grads, left_factors, right_factors, chunk, before):
    chunk_slots, rows_block, cols_block = grads.shape

    def pick(*tail):
        return pl.BlockSpec((chunk_slots,) + tail, lambda g: (chunk, 0, 0))

    def whole(*tail):
        return pl.BlockSpec((chunk_slots,) + tail, lambda g: (0, 0, 0))

    chained = before is not None
    specs = [
        whole(rows_block, cols_block),
        pick(rows_block, rows_block),
        pick(cols_block, cols_block),
    ]
    operands = [grads, left_factors, right_factors]
    aliases = {}
    if chained:
        specs += [pl.BlockSpec(memory_space=pl.ANY)] * 2
        operands += list(before)
        aliases = {3: 0, 4: 1}

    def scratch(order):
        square = (chunk_slots, order, order)
        return [
            pltpu.VMEM(square, jnp.bfloat16),
            pltpu.VMEM(square, jnp.bfloat16),
            pltpu.VMEM(square, jnp.float32),
        ]

    return pl.pallas_call(
        functools.partial(block_kernel, chunk_slots=chunk_slots, chained=chained),
        grid=(1,),
        out_shape=(
            jax.ShapeDtypeStruct(left_factors.shape, jnp.float32),
            jax.ShapeDtypeStruct(right_factors.shape, jnp.float32),
            jax.ShapeDtypeStruct(grads.shape, jnp.bfloat16),
        ),
        in_specs=specs,
        out_specs=(
            pick(rows_block, rows_block),
            pick(cols_block, cols_block),
            whole(rows_block, cols_block),
        ),
        scratch_shapes=scratch(rows_block) + scratch(cols_block),
        input_output_aliases=aliases,
        compiler_params=pltpu.CompilerParams(vmem_limit_bytes=VMEM_LIMIT),
        cost_estimate=pl.CostEstimate(
            flops=2 * chunk_slots * rows_block**3 * 4 * ITERS,
            bytes_accessed=chunk_slots * rows_block * rows_block * 8,
            transcendentals=0,
        ),
    )(*operands)


def pick_kernel(dev_ref, pos_ref, sub_ref, *refs, shape, chunk_slots, piece_rows, cols_block):
    sources, out_ref, sem = refs[:-2], refs[-2], refs[-1]
    projections, per_shard, col_blocks = shape
    index = 0
    for projection in range(projections):
        for piece in range(per_shard):
            for column in range(col_blocks):
                dest = out_ref.at[
                    projection,
                    pl.ds(piece * piece_rows, piece_rows),
                    pl.ds(column * cols_block, cols_block),
                ]
                rows = pl.ds(pl.multiple_of(sub_ref[piece] * piece_rows, piece_rows), piece_rows)
                for chunk, source in enumerate(sources):

                    @pl.when(pos_ref[index] // chunk_slots == chunk)
                    def _():
                        pltpu.make_async_copy(
                            source.at[dev_ref[index], pos_ref[index] % chunk_slots, rows], dest, sem.at[index]
                        ).start()

                index += 1
    index = 0
    for projection in range(projections):
        for piece in range(per_shard):
            for column in range(col_blocks):
                dest = out_ref.at[
                    projection,
                    pl.ds(piece * piece_rows, piece_rows),
                    pl.ds(column * cols_block, cols_block),
                ]
                pltpu.make_async_copy(
                    sources[0].at[0, 0, pl.ds(0, piece_rows)], dest, sem.at[index]
                ).wait()
                index += 1


def pick_rows(gathered, owner_table, shard_rows, row_blocks, col_blocks, slots):
    _, chunk_slots, block_order, cols_block = gathered[0].shape
    piece_rows = min(shard_rows, block_order)
    per_block = block_order // piece_rows
    per_shard = shard_rows // piece_rows
    pieces = lax.axis_index("dp") * per_shard + jnp.arange(per_shard, dtype=jnp.int32)
    wanted = (
        jnp.arange(2, dtype=jnp.int32)[:, None, None] * row_blocks + (pieces // per_block)[None, :, None]
    ) * col_blocks + jnp.arange(col_blocks, dtype=jnp.int32)[None, None, :]
    hits = wanted.reshape(-1)[:, None] == owner_table[None, :]
    where = jnp.sum(
        jnp.where(hits, jnp.arange(owner_table.shape[0], dtype=jnp.int32)[None, :], 0), axis=1, dtype=jnp.int32
    )
    count = 2 * per_shard * col_blocks
    body = functools.partial(
        pick_kernel,
        shape=(2, per_shard, col_blocks),
        chunk_slots=chunk_slots,
        piece_rows=piece_rows,
        cols_block=cols_block,
    )
    shape = (2, shard_rows, col_blocks * cols_block)
    return pl.pallas_call(
        body,
        out_shape=jax.ShapeDtypeStruct(shape, jnp.bfloat16),
        grid_spec=pltpu.PrefetchScalarGridSpec(
            num_scalar_prefetch=3,
            grid=(1,),
            in_specs=[pl.BlockSpec(memory_space=pl.ANY)] * len(gathered),
            out_specs=pl.BlockSpec(shape, lambda g, *_: (0, 0, 0)),
            scratch_shapes=[pltpu.SemaphoreType.DMA((count,))],
        ),
    )(where // slots, where % slots, pieces % per_block, *gathered)


def local(activations, key_value_grads, owner_table, left_factors, right_factors):
    rows_block = left_factors.shape[2]
    cols_block = right_factors.shape[2]
    ranks = lax.axis_size("dp")
    row_blocks = activations.shape[1] // rows_block
    col_blocks = key_value_grads.shape[2] // cols_block
    shard_rows = activations.shape[1] // ranks
    slots = left_factors.shape[1]
    chunk_slots = min(CHUNK_SLOTS, slots)
    cotangents = key_value_grads.reshape(key_value_grads.shape[0], -1)
    grads = []
    for chunk in range(slots // chunk_slots):
        partial = gradient_chunk(
            owner_table, activations, cotangents, chunk, chunk_slots, ranks, rows_block, cols_block, col_blocks
        )
        grads.append(lax.psum_scatter(partial, "dp", scatter_dimension=0, tiled=True)[0])
    before = None
    gathered = []
    for chunk, grad in enumerate(grads):
        left_new, right_new, directions = block_chunk(grad, left_factors[0], right_factors[0], chunk, before)
        before = (left_new, right_new)
        gathered.append(lax.all_gather(directions, "dp", axis=0))
    own_rows = pick_rows(gathered, owner_table, shard_rows, row_blocks, col_blocks, slots)
    update = lax.all_gather(own_rows, "tensor", axis=2, tiled=True)
    return (left_new[None], right_new[None], update)


def solution(mesh):
    in_specs = (
        P("dp", None),
        P("dp", None, "tensor"),
        P(),
        P("tensor", "dp", None, None),
        P("tensor", "dp", None, None),
    )
    out_specs = (P("tensor", "dp", None, None), P("tensor", "dp", None, None), P(None, "dp", None))
    return jax.shard_map(local, mesh=mesh, in_specs=in_specs, out_specs=out_specs, check_vma=False)
```

profile of v0, /device:TPU:0, one launch (start us, length us, event | category | flops | bytes accessed | tf_op | source)
XLA Modules:
  0.0 654.2 jit_solution(9552812316786612481)
XLA Ops:
  7.2 1.7 copy.14
  8.9 8.0 %shard_map.79 = f32[8,2,512,128]{3,2,1,0:T(8,128)} custom-call(s32[64]{0:T(128)} %table_ref.7, bf16[256,8192]{1,0:T(8,128)(2,1)} %act_ref.7, bf16[256,512]{1,0:T(8,128)(2,1)} %bitcast.14), custom_call_target="tpu_custom_call" | custom-call | flops 536870912 | bytes 8388608 | tf_op jit(solution)/shard_map/pallas_call | solution.py:62
  17.0 8.2 %shard_map.78 = f32[8,2,512,128]{3,2,1,0:T(8,128)} custom-call(s32[64]{0:T(128)} %table_ref.7, bf16[256,8192]{1,0:T(8,128)(2,1)} %act_ref.7, bf16[256,512]{1,0:T(8,128)(2,1)} %bitcast.15), custom_call_target="tpu_custom_call" | custom-call | flops 536870912 | bytes 8388608 | tf_op jit(solution)/shard_map/pallas_call | solution.py:62
  25.2 8.5 %shard_map.77 = f32[8,2,512,128]{3,2,1,0:T(8,128)} custom-call(s32[64]{0:T(128)} %table_ref.7, bf16[256,8192]{1,0:T(8,128)(2,1)} %act_ref.7, bf16[256,512]{1,0:T(8,128)(2,1)} %bitcast.16), custom_call_target="tpu_custom_call" | custom-call | flops 536870912 | bytes 8388608 | tf_op jit(solution)/shard_map/pallas_call | solution.py:62
  33.8 8.1 %shard_map.76 = f32[8,2,512,128]{3,2,1,0:T(8,128)} custom-call(s32[64]{0:T(128)} %table_ref.7, bf16[256,8192]{1,0:T(8,128)(2,1)} %act_ref.7, bf16[256,512]{1,0:T(8,128)(2,1)} %bitcast.17), custom_call_target="tpu_custom_call" | custom-call | flops 536870912 | bytes 8388608 | tf_op jit(solution)/shard_map/pallas_call | solution.py:62
  42.0 66.1 %reduce-scatter.11.cloned.1.call-done = f32[1,2,512,128]{3,2,1,0:T(8,128)} async-done(((f32[8,2,512,128]{3,2,1,0:T(8,128)}), f32[1,2,512,128]{3,2,1,0:T(8,128)}) %reduce-scatter.11.cloned.1.call-update) | async-done | bytes 524304 | tf_op jit(solution)/shard_map/reduce_scatter | solution.py:311
  108.1 24.5 %shard_map.80 = (f32[8,512,512]{2,1,0:T(8,128)}, f32[8,128,128]{2,1,0:T(8,128)}, bf16[2,512,128]{2,1,0:T(8,128)(2,1)}) custom-call(f32[2,512,128]{2,1,0:T(8,128)} %bitcast.31, f32[8,512,512]{2,1,0:T(8,128)} %bitcast.23, f32[8,128,128]{2,1,0:T(8,128)} %bitcast.27), custom_call_target="tpu_custom_call" | custom-call | flops 17179869184 | bytes 4194304 | tf_op jit(solution)/shard_map/pallas_call | solution.py:199
  132.6 67.1 %reduce-scatter.9.cloned.1.call-done = f32[1,2,512,128]{3,2,1,0:T(8,128)} async-done(((f32[8,2,512,128]{3,2,1,0:T(8,128)}), f32[1,2,512,128]{3,2,1,0:T(8,128)}) %reduce-scatter.9.cloned.1.call-update) | async-done | bytes 524304 | tf_op jit(solution)/shard_map/reduce_scatter | solution.py:311
  199.7 24.3 %shard_map.81 = (f32[8,512,512]{2,1,0:T(8,128)}, f32[8,128,128]{2,1,0:T(8,128)}, bf16[2,512,128]{2,1,0:T(8,128)(2,1)}) custom-call(f32[2,512,128]{2,1,0:T(8,128)} %bitcast.32, f32[8,512,512]{2,1,0:T(8,128)} %bitcast.24, f32[8,128,128]{2,1,0:T(8,128)} %bitcast.28, ...), custom_call_target="tpu_custom_call", output_to_operand_aliasing={{0}: (3, {}), {1}: (4, {})} | custom-call | flops 17179869184 | bytes 4194304 | tf_op jit(solution)/shard_map/pallas_call | solution.py:199
  224.0 67.3 %reduce-scatter.7.cloned.1.call-done = f32[1,2,512,128]{3,2,1,0:T(8,128)} async-done(((f32[8,2,512,128]{3,2,1,0:T(8,128)}), f32[1,2,512,128]{3,2,1,0:T(8,128)}) %reduce-scatter.7.cloned.1.call-update) | async-done | bytes 524304 | tf_op jit(solution)/shard_map/reduce_scatter | solution.py:311
  291.3 24.5 %shard_map.82 = (f32[8,512,512]{2,1,0:T(8,128)}, f32[8,128,128]{2,1,0:T(8,128)}, bf16[2,512,128]{2,1,0:T(8,128)(2,1)}) custom-call(f32[2,512,128]{2,1,0:T(8,128)} %bitcast.33, f32[8,512,512]{2,1,0:T(8,128)} %bitcast.25, f32[8,128,128]{2,1,0:T(8,128)} %bitcast.29, ...), custom_call_target="tpu_custom_call", output_to_operand_aliasing={{0}: (3, {}), {1}: (4, {})} | custom-call | flops 17179869184 | bytes 4194304 | tf_op jit(solution)/shard_map/pallas_call | solution.py:199
  315.8 67.5 %reduce-scatter.5.cloned.1.call-done = f32[1,2,512,128]{3,2,1,0:T(8,128)} async-done(((f32[8,2,512,128]{3,2,1,0:T(8,128)}), f32[1,2,512,128]{3,2,1,0:T(8,128)}) %reduce-scatter.5.cloned.1.call-update) | async-done | bytes 524304 | tf_op jit(solution)/shard_map/reduce_scatter | solution.py:311
  383.3 24.3 %shard_map.83 = (f32[8,512,512]{2,1,0:T(8,128)}, f32[8,128,128]{2,1,0:T(8,128)}, bf16[2,512,128]{2,1,0:T(8,128)(2,1)}) custom-call(f32[2,512,128]{2,1,0:T(8,128)} %bitcast.34, f32[8,512,512]{2,1,0:T(8,128)} %bitcast.26, f32[8,128,128]{2,1,0:T(8,128)} %bitcast.30, ...), custom_call_target="tpu_custom_call", output_to_operand_aliasing={{0}: (3, {}), {1}: (4, {})} | custom-call | flops 17179869184 | bytes 4194304 | tf_op jit(solution)/shard_map/pallas_call | solution.py:199
  408.3 0.7 all-gather.14.cloned.1.call-update
  409.1 0.7 all-gather.12.cloned.1.call-update
  410.2 0.6 and_select_fusion
  410.8 45.7 %all-gather.18.cloned.1.call-done = bf16[16,512,128]{2,1,0:T(8,128)(2,1)} async-done(((bf16[2,512,128]{2,1,0:T(8,128)(2,1)}), bf16[16,512,128]{2,1,0:T(8,128)(2,1)}) %all-gather.18.cloned.1.call-update) | async-done | bytes 2097168 | tf_op jit(solution)/shard_map/all_gather | solution.py:317
  456.6 49.6 %all-gather.16.cloned.1.call-done = bf16[16,512,128]{2,1,0:T(8,128)(2,1)} async-done(((bf16[2,512,128]{2,1,0:T(8,128)(2,1)}), bf16[16,512,128]{2,1,0:T(8,128)(2,1)}) %all-gather.16.cloned.1.call-update) | async-done | bytes 2097168 | tf_op jit(solution)/shard_map/all_gather | solution.py:317
  506.2 49.8 %all-gather.14.cloned.1.call-done = bf16[16,512,128]{2,1,0:T(8,128)(2,1)} async-done(((bf16[2,512,128]{2,1,0:T(8,128)(2,1)}), bf16[16,512,128]{2,1,0:T(8,128)(2,1)}) %all-gather.14.cloned.1.call-update) | async-done | bytes 2097168 | tf_op jit(solution)/shard_map/all_gather | solution.py:317
  556.0 49.8 %all-gather.12.cloned.1.call-done = bf16[16,512,128]{2,1,0:T(8,128)(2,1)} async-done(((bf16[2,512,128]{2,1,0:T(8,128)(2,1)}), bf16[16,512,128]{2,1,0:T(8,128)(2,1)}) %all-gather.12.cloned.1.call-update) | async-done | bytes 2097168 | tf_op jit(solution)/shard_map/all_gather | solution.py:317
  605.8 0.6 rem.42.sub_ref
  606.3 3.0 shard_map.84
  609.4 33.7 %all-gather.10.cloned.1.call-done = bf16[2,1024,1024]{2,1,0:T(8,128)(2,1)} async-done(((bf16[2,1024,256]{2,1,0:T(8,128)(2,1)}), bf16[2,1024,1024]{2,1,0:T(8,128)(2,1)}) %all-gather.10.cloned.1.call-update) | async-done | bytes 4194320 | tf_op jit(solution)/shard_map/all_gather | solution.py:319
  643.1 4.6 copy.22
  (23 shorter events, 1.4 us)
Async XLA Ops:
  7.2 100.9 %reduce-scatter.11.cloned.1.call-start = ((), (), s32[]{:S(2)}) async-start(), calls=%async_computation.7 | async-start | bytes 4718592 | tf_op jit(solution)/shard_map/reduce_scatter | solution.py:311
  16.9 182.8 %reduce-scatter.9.cloned.1.call-start = ((), (), s32[]{:S(2)}) async-start(), calls=%async_computation.6 | async-start | bytes 4718592 | tf_op jit(solution)/shard_map/reduce_scatter | solution.py:311
  25.2 266.1 %reduce-scatter.7.cloned.1.call-start = ((), (), s32[]{:S(2)}) async-start(), calls=%async_computation.5 | async-start | bytes 4718592 | tf_op jit(solution)/shard_map/reduce_scatter | solution.py:311
  33.8 349.6 %reduce-scatter.5.cloned.1.call-start = ((), (), s32[]{:S(2)}) async-start(), calls=%async_computation.4 | async-start | bytes 4718592 | tf_op jit(solution)/shard_map/reduce_scatter | solution.py:311
  41.9 414.6 %all-gather.18.cloned.1.call-start = ((), (), s32[]{:S(2)}) async-start(), calls=%async_computation.12 | async-start | bytes 2359296 | tf_op jit(solution)/shard_map/all_gather | solution.py:317
  383.3 26.7 %copy-start = (s32[64]{0:T(128)S(1)}, s32[64]{0:T(128)}, u32[]{:S(2)}) copy-start(s32[64]{0:T(128)} %table_ref.7) | copy-start | bytes 772
  407.7 98.5 %all-gather.16.cloned.1.call-start = ((), (), s32[]{:S(2)}) async-start(), calls=%async_computation.11 | async-start | bytes 2359296 | tf_op jit(solution)/shard_map/all_gather | solution.py:317
  408.3 147.7 %all-gather.14.cloned.1.call-start = ((), (), s32[]{:S(2)}) async-start(), calls=%async_computation.10 | async-start | bytes 2359296 | tf_op jit(solution)/shard_map/all_gather | solution.py:317
  409.0 196.7 %all-gather.12.cloned.1.call-start = ((), (), s32[]{:S(2)}) async-start(), calls=%async_computation.9 | async-start | bytes 2359296 | tf_op jit(solution)/shard_map/all_gather | solution.py:317
  409.8 233.3 %all-gather.10.cloned.1.call-start = ((), (), s32[]{:S(2)}) async-start(), calls=%async_computation.8 | async-start | bytes 5242880 | tf_op jit(solution)/shard_map/all_gather | solution.py:319
Sparse Core Ops, SparseCore 0:
  17.1 91.0 reduce-scatter.10
  111.7 87.9 reduce-scatter.8
  203.3 87.9 reduce-scatter.6
  295.4 87.9 reduce-scatter.4
  407.8 48.7 all-gather.17
  458.6 47.6 all-gather.15
  508.3 47.6 all-gather.13
  558.1 47.6 all-gather.11
  609.5 33.5 all-gather.9
where the time goes:
time: 655 us; the launch traced here: 654 us
  waiting for transfers between devices  499 us (76%)
  Pallas kernels  133 us (20%)
  between operations  13.9 us (2%)
  local copies, waits for them, and re-layouts  6.99 us (1%)
    reduce_scatter x4, waiting for transfers between devices, local(): lax.psum_scatter(partial, 'dp', scatter_dimension=0, tiled=True)[0]  268 us
    all_gather x4, waiting for transfers between devices, local(): gathered.append(lax.all_gather(directions, 'dp', axis=0))  195 us
    pallas_call x4, Pallas kernels, block_chunk(): pl.pallas_call(functools.partial(block_kernel, chunk_slots=chunk_slots, c...  97.6 us
    all_gather x1, waiting for transfers between devices, local(): update = lax.all_gather(own_rows, 'tensor', axis=2, tiled=True)  33.7 us
    pallas_call x4, Pallas kernels, gradient_chunk(): pl.pallas_call(body, out_shape=jax.ShapeDtypeStruct((ranks, chunk_slots,...  32.8 us
  transfers between devices with their start and end apart: 9, of which 9 were waited for; matrix products, arithmetic and copies ran while one was open for 0% of the time, Pallas kernels for 15%

commit v1 on v0

--- a/solution.py
+++ b/solution.py
@@ -293,7 +293,7 @@
     )(where // slots, where % slots, pieces % per_block, *gathered)
 
 
-def local(activations, key_value_grads, owner_table, left_factors, right_factors):
+def gathered_path(activations, key_value_grads, owner_table, left_factors, right_factors):
     rows_block = left_factors.shape[2]
     cols_block = right_factors.shape[2]
     ranks = lax.axis_size("dp")
@@ -320,6 +320,516 @@
     return (left_new[None], right_new[None], update)
 
 
+def plan_kernel(table_ref, plan_ref, by_source, by_dest, free_source, free_dest, *, ranks, dest_of):
+    def lowest(mask):
+        found = 0
+        for colour in reversed(range(ranks)):
+            found = jnp.where((mask >> colour) & 1 == 1, colour, found)
+        return found
+
+    def clear(i, carry):
+        by_source[i] = -1
+        by_dest[i] = -1
+        return carry
+
+    lax.fori_loop(0, ranks * ranks, clear, 0)
+    for i in range(ranks):
+        free_source[i] = (1 << ranks) - 1
+        free_dest[i] = (1 << ranks) - 1
+
+    def place(slot, carry):
+        source = slot // ranks
+        dest = dest_of(table_ref[slot])
+        both = free_source[source] & free_dest[dest]
+        shared = both != 0
+        first = lowest(jnp.where(shared, both, free_source[source]))
+        second = lowest(jnp.where(shared, both, free_dest[dest]))
+        moved = by_dest[dest * ranks + first]
+        by_dest[dest * ranks + first] = slot
+        by_source[source * ranks + first] = slot
+        free_source[source] = free_source[source] & ~(1 << first)
+        free_dest[dest] = free_dest[dest] & ~(1 << second)
+
+        @pl.when(jnp.logical_not(shared))
+        def _():
+            by_dest[dest * ranks + second] = moved
+
+        def swap(edge):
+            at_source = edge // ranks
+            other = by_source[at_source * ranks + second]
+            by_source[at_source * ranks + second] = edge
+            by_source[at_source * ranks + first] = other
+
+            @pl.when(other < 0)
+            def _():
+                free_source[at_source] = (free_source[at_source] | (1 << first)) & ~(1 << second)
+
+            at_dest = dest_of(table_ref[jnp.maximum(other, 0)])
+            following = jnp.where(other < 0, -1, by_dest[at_dest * ranks + first])
+
+            @pl.when(other >= 0)
+            def _():
+                by_dest[at_dest * ranks + first] = other
+                by_dest[at_dest * ranks + second] = following
+
+            @pl.when(jnp.logical_and(other >= 0, following < 0))
+            def _():
+                free_dest[at_dest] = (free_dest[at_dest] | (1 << second)) & ~(1 << first)
+
+            return following
+
+        lax.while_loop(lambda edge: edge >= 0, swap, moved)
+        return carry
+
+    lax.fori_loop(0, ranks * ranks, place, 0)
+    for device in range(ranks):
+        for k in range(ranks):
+            plan_ref[device * ranks + k] = by_source[device * ranks + (device ^ k)]
+            plan_ref[(ranks + device) * ranks + k] = by_dest[device * ranks + (device ^ k)]
+
+
+def plan_routes(table, ranks, dest_of):
+    return pl.pallas_call(
+        functools.partial(plan_kernel, ranks=ranks, dest_of=dest_of),
+        out_shape=jax.ShapeDtypeStruct((2 * ranks * ranks,), jnp.int32),
+        in_specs=[pl.BlockSpec(memory_space=pltpu.SMEM)],
+        out_specs=pl.BlockSpec(memory_space=pltpu.SMEM),
+        scratch_shapes=[pltpu.SMEM((ranks * ranks,), jnp.int32)] * 2 + [pltpu.SMEM((ranks,), jnp.int32)] * 2,
+    )(table)
+
+
+def partial_kernel(
+    plan_ref, table_ref, here_ref, act_ref, kv_ref, send_ref, kept_ref, sums, flipped, sem, *, ranks, per_projection, col_blocks, scale
+):
+    step = pl.program_id(0)
+    blocks, cols_block, rows_block = sums.shape
+    group = kv_ref.shape[1] // cols_block
+
+    @pl.when(step == 0)
+    def _():
+        flipped[...] = kv_ref[...].T
+
+    summed = dot(flipped[...], act_ref[...]) * scale
+    sums[pl.ds(step * group, group)] = summed.astype(jnp.bfloat16).reshape(group, cols_block, rows_block)
+
+    @pl.when(step == pl.num_programs(0) - 1)
+    def _():
+        copies = []
+        for i in range(ranks):
+            for relative in [*range(1, ranks, 2), *range(0, ranks, 2)]:
+                owner = here_ref[0] ^ relative
+                block_id = table_ref[plan_ref[owner * ranks + (i + 1) % ranks]]
+                remainder = block_id % per_projection
+                index = (
+                    remainder // col_blocks * group
+                    + block_id // per_projection * col_blocks
+                    + remainder % col_blocks
+                )
+                target = (send_ref if relative % 2 else kept_ref).at[i, relative // 2]
+                copy = pltpu.make_async_copy(sums.at[index], target, sem.at[len(copies)])
+                copy.start()
+                copies.append(copy)
+        for copy in copies:
+            copy.wait()
+
+
+def partial_sums(plan, table, here, activations, cotangents, ranks, rows_block, cols_block, col_blocks):
+    tokens, model = activations.shape
+    row_blocks = model // rows_block
+    blocks = row_blocks * cotangents.shape[1] // cols_block
+    body = functools.partial(
+        partial_kernel,
+        ranks=ranks,
+        per_projection=row_blocks * col_blocks,
+        col_blocks=col_blocks,
+        scale=1.0 / (tokens * ranks),
+    )
+    half = jax.ShapeDtypeStruct((ranks, ranks // 2, cols_block, rows_block), jnp.bfloat16)
+    return pl.pallas_call(
+        body,
+        out_shape=(half, half),
+        grid_spec=pltpu.PrefetchScalarGridSpec(
+            num_scalar_prefetch=3,
+            grid=(row_blocks,),
+            in_specs=[
+                pl.BlockSpec((tokens, rows_block), lambda r, *_: (0, r)),
+                pl.BlockSpec(cotangents.shape, lambda r, *_: (0, 0), pipeline_mode=pl.Buffered(1)),
+            ],
+            out_specs=[pl.BlockSpec(memory_space=pl.ANY)] * 2,
+            scratch_shapes=[
+                pltpu.VMEM((blocks, cols_block, rows_block), jnp.bfloat16),
+                pltpu.VMEM(cotangents.shape[::-1], jnp.bfloat16),
+                pltpu.SemaphoreType.DMA((ranks * ranks,)),
+            ],
+        ),
+        compiler_params=pltpu.CompilerParams(vmem_limit_bytes=VMEM_LIMIT),
+    )(plan, table, here, activations, cotangents)
+
+
+def flip(index, mask, size):
+    flipped, bit = 0, 1
+    while bit < size:
+        flipped = flipped + (index // bit + mask // bit) % 2 * bit
+        bit *= 2
+    return flipped
+
+
+def main_kernel(
+    plan_ref, send_ref, kept_ref, left_ref, right_ref, left_out, right_out, held_ref,
+    lefts, rights, left_stage, right_stage, kept, came_y, own, send_z, came_z, ways, arrived, ordered,
+    ml, fl, xl, mr, fr, xr,
+    load_sem, out_sem, local_sem, y_send, y_recv, z_send, z_recv, way_send, way_recv, dp_send, dp_recv, tp_send, tp_recv,
+    *, ranks, shards, pair,
+):
+    me, column = lax.axis_index("dp"), lax.axis_index("tensor")
+    mesh_id = pl.DeviceIdType.MESH
+    half = ranks // 2
+    bits = [1 << i for i in reversed(range(shards.bit_length() - 1))]
+
+    loads = []
+    for i in range(ranks):
+        loads.append(pltpu.make_async_copy(kept_ref.at[i], kept.at[i], load_sem.at[0, i]))
+        loads.append(pltpu.make_async_copy(left_ref.at[i], lefts.at[i], load_sem.at[1, i]))
+        loads.append(pltpu.make_async_copy(right_ref.at[i], rights.at[i], load_sem.at[2, i]))
+    for copy in loads:
+        copy.start()
+
+    barrier = pltpu.get_barrier_semaphore()
+    for q in range(1, ranks):
+        pl.semaphore_signal(barrier, inc=1, device_id=(flip(me, q, ranks), column), device_id_type=mesh_id)
+    for bit in bits:
+        pl.semaphore_signal(barrier, inc=1, device_id=(me, flip(column, bit, shards)), device_id_type=mesh_id)
+    pl.semaphore_wait(barrier, ranks - 1 + len(bits))
+
+    def along_dp(source, target, sent, received, mask):
+        return pltpu.make_async_remote_copy(
+            src_ref=source,
+            dst_ref=target,
+            send_sem=sent,
+            recv_sem=received,
+            device_id=(flip(me, mask, ranks), column),
+            device_id_type=mesh_id,
+        )
+
+    def first_hop(i):
+        return along_dp(send_ref.at[i], came_y.at[i], y_send.at[i], y_recv.at[i], 1)
+
+    def second_hop(i, q):
+        return along_dp(send_z.at[i, q - 1], came_z.at[i, q - 1], z_send.at[i, q - 1], z_recv.at[i, q - 1], 2 * q)
+
+    def way(i):
+        k = (i + 1) % ranks
+        return along_dp(ways.at[i], arrived.at[i], way_send.at[i], way_recv.at[i], k)
+
+    for i in range(ranks):
+        first_hop(i).start()
+    for copy in loads:
+        copy.wait()
+
+    def fold(i):
+        first_hop(i).wait_recv()
+        own[i] = kept[i, 0].astype(jnp.float32) + came_y[i, 0].astype(jnp.float32)
+        for q in range(1, half):
+            summed = kept[i, q].astype(jnp.float32) + came_y[i, q].astype(jnp.float32)
+            send_z[i, q - 1] = summed.astype(jnp.bfloat16)
+
+    def send(i):
+        for q in range(1, half):
+            second_hop(i, q).start()
+
+    for i in range(pair):
+        fold(i)
+    for i in range(pair):
+        send(i)
+
+    def outs(p):
+        copies = []
+        for k in range(pair):
+            i = p * pair + k
+            copies.append(pltpu.make_async_copy(left_stage.at[k], left_out.at[i], out_sem.at[0, k]))
+            copies.append(pltpu.make_async_copy(right_stage.at[k], right_out.at[i], out_sem.at[1, k]))
+        return copies
+
+    def group(p, more):
+        if more:
+            fold((p + 1) * pair)
+            send((p + 1) * pair)
+        groups = []
+        for k in range(pair):
+            i = p * pair + k
+            slot = plan_ref[me * ranks + (i + 1) % ranks] % ranks
+            for q in range(1, half):
+                second_hop(i, q).wait_recv()
+            flipped = own[i]
+            for q in range(1, half):
+                flipped = flipped + came_z[i, q - 1].astype(jnp.float32)
+            own[i] = flipped
+            grad = flipped.T
+            high, low = halves(grad)
+            high_t, low_t = halves(flipped)
+            wide = jnp.concatenate([high, high, low], axis=1)
+            wide_t = jnp.concatenate([high_t, high_t, low_t], axis=1)
+            tall = jnp.concatenate([high, low, high], axis=0)
+            tall_t = jnp.concatenate([high_t, low_t, high_t], axis=0)
+            left_new = MOMENT_DECAY * lefts[slot] + (1.0 - MOMENT_DECAY) * dot(wide, tall_t)
+            right_new = MOMENT_DECAY * rights[slot] + (1.0 - MOMENT_DECAY) * dot(wide_t, tall)
+            left_stage[k] = left_new
+            right_stage[k] = right_new
+            begin_root(left_new, ml.at[k], fl.at[k], xl.at[k])
+            begin_root(right_new, mr.at[k], fr.at[k], xr.at[k])
+            groups.append((ml.at[k], fl.at[k], xl.at[k]))
+            groups.append((mr.at[k], fr.at[k], xr.at[k]))
+        for copy in outs(p):
+            copy.start()
+
+        def step(_, carry):
+            root_steps(groups)
+            return carry
+
+        lax.fori_loop(0, (ITERS - 1) // 2, step, 0)
+        for k in range(1, pair if more else 1):
+            fold((p + 1) * pair + k)
+            send((p + 1) * pair + k)
+        lax.fori_loop((ITERS - 1) // 2, ITERS - 1, step, 0)
+        for k in range(pair):
+            i = p * pair + k
+            high, low = halves(own[i].T)
+            tall = jnp.concatenate([high, low, high], axis=0)
+            root_high, root_low = halves(xl[k])
+            half_pre = dot(jnp.concatenate([root_high, root_high, root_low], axis=1), tall)
+            half_high, half_low = halves(half_pre)
+            right_high, right_low = halves(xr[k])
+            precond = dot(
+                jnp.concatenate([half_high, half_high, half_low], axis=1),
+                jnp.concatenate([right_high, right_low, right_high], axis=0),
+            )
+            mean = total(precond * precond) / precond.size
+            ways[i] = (precond / jnp.sqrt(mean + 1e-06)).astype(jnp.bfloat16)
+        for copy in outs(p):
+            copy.wait()
+        for k in range(pair if more else pair - 1):
+            way(p * pair + k).start()
+
+    def grouped(p, carry):
+        group(p, True)
+        return carry
+
+    last = ranks // pair - 1
+    lax.fori_loop(0, last, grouped, 0)
+    group(last, False)
+    arrived[ranks - 1] = ways[ranks - 1]
+    for i in range(ranks - 1):
+        way(i).wait_recv()
+
+    hops, relays = {}, {}
+    for q in [*range(1, ranks), 0]:
+        came_from = flip(plan_ref[(ranks + flip(me, q, ranks)) * ranks + q] // ranks, me, ranks)
+        ordered[q] = arrived[(came_from + ranks - 1) % ranks]
+        if q > 0:
+            hops[q] = along_dp(ordered.at[q], held_ref.at[0, q], dp_send.at[q], dp_recv.at[q], q)
+            hops[q].start()
+    mine = pltpu.make_async_copy(ordered.at[0], held_ref.at[0, 0], local_sem)
+    mine.start()
+
+    def relay(origin, q):
+        for bit in bits:
+            if origin % (2 * bit) == 0:
+                copy = pltpu.make_async_remote_copy(
+                    src_ref=ordered.at[q] if origin == 0 and q == 0 else held_ref.at[origin, q],
+                    dst_ref=held_ref.at[origin + bit, q],
+                    send_sem=tp_send.at[origin + bit, q],
+                    recv_sem=tp_recv.at[origin + bit, q],
+                    device_id=(me, flip(column, bit, shards)),
+                    device_id_type=mesh_id,
+                )
+                copy.start()
+                relays[origin + bit, q] = copy
+
+    before = None
+    for q in range(ranks):
+        if q > 0:
+            hops[q].wait_recv()
+        relay(0, q)
+        if before is not None:
+            for origin in range(1, shards):
+                relays[origin, before].wait_recv()
+                relay(origin, before)
+        before = q
+    for origin in range(1, shards):
+        relays[origin, before].wait_recv()
+        relay(origin, before)
+    mine.wait()
+    for i in range(ranks):
+        first_hop(i).wait_send()
+        for q in range(1, half):
+            second_hop(i, q).wait_send()
+        if i < ranks - 1:
+            way(i).wait_send()
+    for copy in [*hops.values(), *relays.values()]:
+        copy.wait_send()
+
+
+def main_step(plan, sends, kept, left_factors, right_factors, shards):
+    ranks, half, cols_block, rows_block = sends.shape
+    pair = CHUNK_SLOTS
+    f32, bf16 = jnp.float32, jnp.bfloat16
+    anywhere = pl.BlockSpec(memory_space=pl.ANY)
+
+    def squares(order):
+        square = (pair, order, order)
+        return [pltpu.VMEM(square, bf16), pltpu.VMEM(square, bf16), pltpu.VMEM(square, f32)]
+
+    flat, tall = (cols_block, rows_block), (rows_block, cols_block)
+    dma = pltpu.SemaphoreType.DMA
+    return pl.pallas_call(
+        functools.partial(main_kernel, ranks=ranks, shards=shards, pair=pair),
+        out_shape=(
+            jax.ShapeDtypeStruct(left_factors.shape, f32),
+            jax.ShapeDtypeStruct(right_factors.shape, f32),
+            jax.ShapeDtypeStruct((shards, ranks) + tall, bf16),
+        ),
+        in_specs=[pl.BlockSpec(memory_space=pltpu.SMEM)] + [anywhere] * 4,
+        out_specs=(anywhere,) * 3,
+        scratch_shapes=[
+            pltpu.VMEM(left_factors.shape, f32),
+            pltpu.VMEM(right_factors.shape, f32),
+            pltpu.VMEM((pair,) + left_factors.shape[1:], f32),
+            pltpu.VMEM((pair,) + right_factors.shape[1:], f32),
+            pltpu.VMEM((ranks, half) + flat, bf16),
+            pltpu.VMEM((ranks, half) + flat, bf16),
+            pltpu.VMEM((ranks,) + flat, f32),
+            pltpu.VMEM((ranks, half - 1) + flat, bf16),
+            pltpu.VMEM((ranks, half - 1) + flat, bf16),
+            pltpu.VMEM((ranks,) + tall, bf16),
+            pltpu.VMEM((ranks,) + tall, bf16),
+            pltpu.VMEM((ranks,) + tall, bf16),
+            *squares(rows_block),
+            *squares(cols_block),
+            dma((3, ranks)),
+            dma((2, pair)),
+            dma,
+            dma((ranks,)),
+            dma((ranks,)),
+            dma((ranks, half - 1)),
+            dma((ranks, half - 1)),
+            dma((ranks,)),
+            dma((ranks,)),
+            dma((ranks,)),
+            dma((ranks,)),
+            dma((shards, ranks)),
+            dma((shards, ranks)),
+        ],
+        compiler_params=pltpu.CompilerParams(
+            collective_id=0, has_side_effects=True, vmem_limit_bytes=VMEM_LIMIT
+        ),
+    )(plan, sends, kept, left_factors, right_factors)
+
+
+def place_kernel(plan_ref, here_ref, left_ref, right_ref, left_out, right_out):
+    left_out[...] = left_ref[...]
+    right_out[...] = right_ref[...]
+
+
+def place_slots(plan, here, left_new, right_new):
+    ranks = left_new.shape[0]
+
+    def slot_of(i, plan_ref, here_ref):
+        return (plan_ref[here_ref[0] * ranks + (i + 1) % ranks] % ranks, 0, 0)
+
+    def block(x):
+        return (1,) + x.shape[1:]
+
+    return pl.pallas_call(
+        place_kernel,
+        out_shape=(
+            jax.ShapeDtypeStruct(left_new.shape, jnp.float32),
+            jax.ShapeDtypeStruct(right_new.shape, jnp.float32),
+        ),
+        grid_spec=pltpu.PrefetchScalarGridSpec(
+            num_scalar_prefetch=2,
+            grid=(ranks,),
+            in_specs=[
+                pl.BlockSpec(block(left_new), lambda i, *_: (i, 0, 0)),
+                pl.BlockSpec(block(right_new), lambda i, *_: (i, 0, 0)),
+            ],
+            out_specs=(pl.BlockSpec(block(left_new), slot_of), pl.BlockSpec(block(right_new), slot_of)),
+        ),
+    )(plan, here, left_new, right_new)
+
+
+def assemble_kernel(plan_ref, table_ref, here_ref, held_ref, out_ref, sem, *, per_projection, col_blocks):
+    shards, ranks, rows_block, cols_block = held_ref.shape
+    shard_rows = out_ref.shape[1]
+    copies = []
+    for q in range(ranks):
+        block_id = table_ref[plan_ref[(ranks + here_ref[0]) * ranks + q]]
+        remainder = block_id % per_projection
+        row_start = pl.multiple_of(remainder // col_blocks * rows_block % shard_rows, rows_block)
+        for origin in range(shards):
+            shard = here_ref[1] ^ origin
+            col_start = pl.multiple_of((shard * col_blocks + remainder % col_blocks) * cols_block, cols_block)
+            source = held_ref.at[origin, q]
+            target = out_ref.at[
+                block_id // per_projection, pl.ds(row_start, rows_block), pl.ds(col_start, cols_block)
+            ]
+            copies.append(pltpu.make_async_copy(source, target, sem.at[len(copies)]))
+            copies[-1].start()
+    for copy in copies:
+        copy.wait()
+
+
+def assemble(plan, table, here, held, projections, shard_rows, per_projection, col_blocks):
+    shards, ranks, _, cols_block = held.shape
+    shape = (projections, shard_rows, shards * col_blocks * cols_block)
+    return pl.pallas_call(
+        functools.partial(assemble_kernel, per_projection=per_projection, col_blocks=col_blocks),
+        out_shape=jax.ShapeDtypeStruct(shape, jnp.bfloat16),
+        grid_spec=pltpu.PrefetchScalarGridSpec(
+            num_scalar_prefetch=3,
+            grid=(1,),
+            in_specs=[pl.BlockSpec(memory_space=pl.ANY)],
+            out_specs=pl.BlockSpec(shape, lambda g, *_: (0, 0, 0)),
+            scratch_shapes=[pltpu.SemaphoreType.DMA((shards * ranks,))],
+        ),
+        compiler_params=pltpu.CompilerParams(vmem_limit_bytes=VMEM_LIMIT),
+    )(plan, table, here, held)
+
+
+def routed_path(activations, key_value_grads, owner_table, left_factors, right_factors):
+    rows_block = left_factors.shape[2]
+    cols_block = right_factors.shape[2]
+    ranks = lax.axis_size("dp")
+    shards = lax.axis_size("tensor")
+    projections = key_value_grads.shape[1]
+    col_blocks = key_value_grads.shape[2] // cols_block
+    per_projection = activations.shape[1] // rows_block * col_blocks
+    shard_rows = activations.shape[1] // ranks
+    cotangents = key_value_grads.reshape(key_value_grads.shape[0], -1)
+    here = jnp.stack([lax.axis_index("dp"), lax.axis_index("tensor")]).astype(jnp.int32)
+
+    def dest_of(block_id):
+        return block_id % per_projection // col_blocks * rows_block // shard_rows
+
+    plan = plan_routes(owner_table, ranks, dest_of)
+    sends, kept = partial_sums(
+        plan, owner_table, here, activations, cotangents, ranks, rows_block, cols_block, col_blocks
+    )
+    left_new, right_new, held = main_step(plan, sends, kept, left_factors[0], right_factors[0], shards)
+    left_new, right_new = place_slots(plan, here, left_new, right_new)
+    update = assemble(plan, owner_table, here, held, projections, shard_rows, per_projection, col_blocks)
+    return (left_new[None], right_new[None], update)
+
+
+def local(activations, key_value_grads, owner_table, left_factors, right_factors):
+    ranks, shards = lax.axis_size("dp"), lax.axis_size("tensor")
+    shard_rows = activations.shape[1] // ranks
+    whole_blocks = shard_rows % left_factors.shape[2] == 0
+    powers = ranks & (ranks - 1) == 0 and shards & (shards - 1) == 0
+    one_each = left_factors.shape[1] == ranks and ranks % CHUNK_SLOTS == 0
+    path = routed_path if whole_blocks and powers and one_each else gathered_path
+    return path(activations, key_value_grads, owner_table, left_factors, right_factors)
+
+
 def solution(mesh):
     in_specs = (
         P("dp", None),

time: 655 us -> 241 us (0.37)
  waiting for transfers between devices: 499 us -> 0 us
  Pallas kernels: 133 us -> 237 us
  between operations: 13.9 us -> 0.82 us
    reduce_scatter x4 -> x0, waiting for transfers between devices: 268 us -> none  [local(): lax.psum_scatter(partial, 'dp', scatter_dimension=0, tiled=True)[0]]
    all_gather x5 -> x0, waiting for transfers between devices: 229 us -> none  [the longest x4 195 us: local(): gathered.append(lax.all_gather(directions, 'dp', axis=0))]
    pallas_call x9 -> x5, Pallas kernels: 133 us -> 237 us  [the longest x1 200 us: main_step(): pl.pallas_call(functools.partial(main_kernel, ranks=ranks, shards=shards,...]
  transfers between devices with their start and end apart: 9 -> 0, of which waited for: 9 -> 0; matrix products, arithmetic and copies ran while one was open for 0% -> 0% of each run, Pallas kernels for 15% -> 0%
where the time goes in v1:
time: 241 us; the launch traced here: 240 us
  Pallas kernels  237 us (98%)
    pallas_call x1, Pallas kernels, main_step(): pl.pallas_call(functools.partial(main_kernel, ranks=ranks, shards=shards,...  200 us
    pallas_call x1, Pallas kernels, partial_sums(): pl.pallas_call(body, out_shape=(half, half), grid_spec=pltpu.PrefetchScal...  15.2 us
    pallas_call x1, Pallas kernels, place_slots(): pl.pallas_call(place_kernel, out_shape=(jax.ShapeDtypeStruct(left_new.sha...  9.88 us
    pallas_call x1, Pallas kernels, plan_routes(): pl.pallas_call(functools.partial(plan_kernel, ranks=ranks, dest_of=dest_o...  5.93 us
    pallas_call x1, Pallas kernels, assemble(): pl.pallas_call(functools.partial(assemble_kernel, per_projection=per_proj...  5.27 us

profile of v1, /device:TPU:0, one launch (start us, length us, event | category | flops | bytes accessed | tf_op | source)
XLA Modules:
  0.0 239.8 jit_solution(16087127603379920171)
XLA Ops:
  0.6 0.7 pad_add_fusion.here_ref
  1.3 5.9 %shard_map.76.plan_ref = s32[128]{0:T(128)} custom-call(s32[64]{0:T(128)} %table_ref.5), custom_call_target="tpu_custom_call" | custom-call | tf_op jit(solution)/shard_map/pallas_call | solution.py:392
  7.2 1.7 copy.8
  8.9 15.2 %shard_map.77 = (bf16[8,4,128,512]{3,2,1,0:T(8,128)(2,1)}, bf16[8,4,128,512]{3,2,1,0:T(8,128)(2,1)}) custom-call(s32[128]{0:T(128)} %shard_map.76.plan_ref, s32[64]{0:T(128)} %table_ref.5, s32[2]{0:T(128)} %pad_add_fusion.here_ref, bf16[256,8192]{1,0:T(8,128)(2,1)} %act_ref.1, bf16[256,512]{1,0:T(8,128)(2,1)} %bitcast.9), custom_call_target="tpu_custom_call" | custom-call | tf_op jit(solution)/shard_map/pallas_call | solution.py:448
  24.1 200.3 %shard_map.78 = (f32[8,512,512]{2,1,0:T(8,128)}, f32[8,128,128]{2,1,0:T(8,128)}, bf16[4,8,512,128]{3,2,1,0:T(8,128)(2,1)}) custom-call(s32[128]{0:T(128)} %shard_map.76.plan_ref, bf16[8,4,128,512]{3,2,1,0:T(8,128)(2,1)} %get-tuple-element.10.send_ref, bf16[8,4,128,512]{3,2,1,0:T(8,128)(2,1)} %get-tuple-element.11.kept_ref, f32[8,512,512]{2,1,0:T(8,128)} %bitcast.8, ...), custom_call_target="tpu_custom_call" | custom-call | tf_op jit(solution)/shard_map/pallas_call | solution.py:684
  224.4 9.9 %shard_map.79 = (f32[8,512,512]{2,1,0:T(8,128)}, f32[8,128,128]{2,1,0:T(8,128)}) custom-call(s32[128]{0:T(128)} %shard_map.76.plan_ref, s32[2]{0:T(128)} %pad_add_fusion.here_ref, f32[8,512,512]{2,1,0:T(8,128)} %get-tuple-element.12.left_ref, f32[8,128,128]{2,1,0:T(8,128)} %get-tuple-element.13.right_ref), custom_call_target="tpu_custom_call" | custom-call | tf_op jit(solution)/shard_map/pallas_call | solution.py:742
  234.3 5.3 %shard_map.80 = bf16[2,1024,1024]{2,1,0:T(8,128)(2,1)} custom-call(s32[128]{0:T(128)} %shard_map.76.plan_ref, s32[64]{0:T(128)} %table_ref.5, s32[2]{0:T(128)} %pad_add_fusion.here_ref, bf16[4,8,512,128]{3,2,1,0:T(8,128)(2,1)} %get-tuple-element.16.held_ref), custom_call_target="tpu_custom_call" | custom-call | tf_op jit(solution)/shard_map/pallas_call | solution.py:784
